TPU v7x, 256 devices: a whole 4x4x8 slice. The times are simulated.
256 devices in a mesh: seq: 32 (over z, x), head: 8 (over y, core).
Axes of the slice: x: 4, y: 4, z: 8, core: 2. Of those that a mesh axis runs over, the one named last changes fastest.
Arguments:
- block_input: bfloat16 [8, 256, 5120], P(None, 'seq'), may hold values from -6 to 6
- accepted: bfloat16 [8, 256, 5120], P(None, 'seq'), may hold values from -6 to 6
- accept_mask: int32 [8, 256], P(None, 'seq'), may hold values 0 or 1
- cache_lengths: int32 [8], replicated, may hold values from 1 to 8192, as said below
- page_table: int32 [512], replicated, may hold values from 0 to 511, each once
- norm_gain: float32 [5120], replicated, may hold values from 0.1 to 1.9
- w_query: bfloat16 [5120, 3072], P('seq', 'head'), may hold values from -0.078125 to 0.078125
- w_key: bfloat16 [5120, 3072], P('seq', 'head'), may hold values from -0.078125 to 0.078125
- w_value: bfloat16 [5120, 3072], P('seq', 'head'), may hold values from -0.25 to 0.25
- w_out: bfloat16 [5120, 3072], P('seq', 'head'), may hold values from -0.109375 to 0.109375
- key_cache: bfloat16 [512, 128, 3072], P('seq', None, 'head')
- value_cache: bfloat16 [512, 128, 3072], P('seq', None, 'head'), may hold values from -18 to 18
Outputs:
- first_out: bfloat16 [8, 256, 5120], P(None, 'seq', 'head')
- second_out: bfloat16 [8, 256, 5120], P(None, 'seq', 'head')
Inputs may be any that keep to these rules, and one draw needn't show every extreme that they name: `cache_lengths`: max(1, 4) requests, chosen at random, hold (63) * 128 + 1 to 8192 cached tokens, one of them exactly 8192; the others hold 1 to 256. `page_table`: A permutation of the 512 pool pages; entry r * 64 + j is the pool page of cached positions j * 128 to (j + 1) * 128 - 1 of request r.
All inputs are finite; a program needn't handle non-finite values. No bound on the sum of `accept_mask` on one device may be relied on, other than what follows from the above.
Results may differ from a plain program's by a relative error of at most 0.024.
The roundings to bfloat16 on the way count: a program that leaves them out, or rounds other values in their place, can miss the bound.
Values may be sent and summed in bfloat16 or wider, within the bound.
A program may use at most 128 MiB of HBM per device.

v0:
```python
import jax
import jax.numpy as jnp
from jax import lax
from jax.sharding import PartitionSpec as P

HD = 128
PAGE = 128
MAXP = 64
masked_score = -1e30


def rotate(vectors, positions):
    half_width = vectors.shape[-1] // 2
    frequency = 10000.0 ** (-(jnp.arange(half_width).astype(jnp.float32) * 2.0) / vectors.shape[-1])
    angles = positions[..., None, None] * frequency
    cosine = jnp.cos(angles)
    sine_part = jnp.sin(angles)
    front_half = vectors[..., :half_width]
    back_half = vectors[..., half_width:]
    return jnp.concatenate(
        [front_half * cosine - back_half * sine_part, back_half * cosine + front_half * sine_part],
        axis=-1,
    )


def normalize(inputs, norm_gain):
    widened = inputs.astype(jnp.float32)
    inverse = lax.rsqrt(jnp.mean(widened * widened, axis=-1, keepdims=True) + 1e-05)
    return (widened * inverse * norm_gain).astype(jnp.bfloat16)


def per_device(
    block_input,
    accepted,
    accept_mask,
    cache_lengths,
    page_table,
    norm_gain,
    w_query,
    w_key,
    w_value,
    w_out,
    key_cache,
    value_cache,
):
    seq_place = lax.axis_index("seq")
    requests, part_len, model_width = block_input.shape
    local_width = w_query.shape[1]
    local_heads = local_width // HD
    row_count = 2 * requests * part_len
    swapped = jnp.where(accept_mask[:, :, None] == 1, accepted, block_input)
    token_rows = normalize(jnp.stack([block_input, swapped]), norm_gain).reshape(
        row_count, model_width
    )
    full_query, full_key, full_value, out_weight = (
        lax.all_gather(w_query, "seq", axis=0, tiled=True),
        lax.all_gather(w_key, "seq", axis=0, tiled=True),
        lax.all_gather(w_value, "seq", axis=0, tiled=True),
        lax.all_gather(w_out, "seq", axis=0, tiled=True),
    )
    query_rows = jnp.dot(token_rows, full_query, preferred_element_type=jnp.float32)
    key_rows = jnp.dot(token_rows, full_key, preferred_element_type=jnp.float32)
    value_rows = jnp.dot(token_rows, full_value, preferred_element_type=jnp.float32)
    positions = (
        cache_lengths[:, None]
        + seq_place * part_len
        + jnp.arange(part_len, dtype=jnp.int32)[None, :]
    ).astype(jnp.float32)
    shaped = (2, requests, part_len, local_heads, HD)
    new_queries = rotate(query_rows.reshape(shaped), positions).astype(jnp.bfloat16)
    new_keys = rotate(key_rows.reshape(shaped), positions).astype(jnp.bfloat16)
    new_values = value_rows.reshape(shaped).astype(jnp.bfloat16)
    every_query = lax.all_gather(new_queries, "seq", axis=2, tiled=True)
    pages_here = key_cache.shape[0]
    page_ids = seq_place * pages_here + jnp.arange(pages_here, dtype=jnp.int32)
    table_slots = jnp.arange(page_table.shape[0], dtype=jnp.int32)
    slot_of = jnp.sum(
        jnp.where(page_table[None, :] == page_ids[:, None], table_slots[None, :], 0), axis=1
    )
    page_owner = slot_of // MAXP
    owner_match = page_owner[:, None] == jnp.arange(requests, dtype=jnp.int32)[None, :]
    owner_length = jnp.sum(jnp.where(owner_match, cache_lengths[None, :], 0), axis=1)
    offsets = (slot_of % MAXP)[:, None] * PAGE + jnp.arange(PAGE, dtype=jnp.int32)[None, :]
    live_mask = (offsets < owner_length[:, None])[:, None, None, :]
    owner_hot = owner_match.astype(jnp.float32)
    cached_keys = key_cache.reshape(pages_here, PAGE, local_heads, HD)
    cached_values = value_cache.reshape(pages_here, PAGE, local_heads, HD)
    score_scale = HD ** (-0.5)

    def local_part(pass_items):
        pass_queries, pass_keys, pass_values = pass_items
        page_queries = jnp.take(pass_queries, page_owner, axis=0)
        scores = (
            jnp.einsum(
                "pqhd,pkhd->pqhk", page_queries, cached_keys, preferred_element_type=jnp.float32
            )
            * score_scale
        )
        scores = jnp.where(live_mask, scores, masked_score)
        page_peak = jnp.max(scores, axis=-1)
        weights = jnp.where(live_mask, jnp.exp(scores - page_peak[..., None]), 0.0)
        page_total = jnp.sum(weights, axis=-1)
        page_out = jnp.einsum(
            "pqhk,pkhd->pqhd",
            weights.astype(jnp.bfloat16),
            cached_values,
            preferred_element_type=jnp.float32,
        )
        owner_peak = jnp.max(
            jnp.where(owner_match[:, :, None, None], page_peak[:, None], masked_score), axis=0
        )
        factor = jnp.exp(page_peak - jnp.take(owner_peak, page_owner, axis=0))
        cache_total = jnp.einsum(
            "pr,pqh->rqh", owner_hot, page_total * factor, precision=lax.Precision.HIGHEST
        )
        cache_out = jnp.einsum(
            "pr,pqhd->rqhd",
            owner_hot,
            page_out * factor[..., None],
            precision=lax.Precision.HIGHEST,
        )
        block_scores = (
            jnp.einsum(
                "rqhd,rkhd->rqhk", pass_queries, pass_keys, preferred_element_type=jnp.float32
            )
            * score_scale
        )
        block_peak = jnp.max(block_scores, axis=-1)
        block_weights = jnp.exp(block_scores - block_peak[..., None])
        block_total = jnp.sum(block_weights, axis=-1)
        block_out = jnp.einsum(
            "rqhk,rkhd->rqhd",
            block_weights,
            pass_values.astype(jnp.float32),
            precision=lax.Precision.HIGHEST,
        )
        row_peak = jnp.maximum(owner_peak, block_peak)
        cache_factor = jnp.exp(owner_peak - row_peak)
        block_factor = jnp.exp(block_peak - row_peak)
        joined_total = cache_total * cache_factor + block_total * block_factor
        joined_out = cache_out * cache_factor[..., None] + block_out * block_factor[..., None]
        return (row_peak, joined_total, joined_out)

    row_peak, row_total, row_out = lax.map(local_part, (every_query, new_keys, new_values))
    overall = lax.pmax(row_peak, "seq")
    rescale = jnp.exp(row_peak - overall)
    summed_out, summed_total = (
        lax.psum_scatter(row_out * rescale[..., None], "seq", scatter_dimension=2, tiled=True),
        lax.psum_scatter(row_total * rescale, "seq", scatter_dimension=2, tiled=True),
    )
    context = (
        (summed_out / summed_total[..., None]).astype(jnp.bfloat16).reshape(row_count, local_width)
    )
    partial_value = lax.dot_general(
        context, out_weight, (((1,), (1,)), ((), ())), preferred_element_type=jnp.float32
    )
    own_share = lax.psum_scatter(partial_value, "head", scatter_dimension=1, tiled=True).astype(
        jnp.bfloat16
    )
    result = own_share.reshape(2, requests, part_len, own_share.shape[1])
    return (result[0], result[1])


def solution(mesh):
    placed = (
        P(None, "seq", None),
        P(None, "seq", None),
        P(None, "seq"),
        P(),
        P(),
        P(),
        P("seq", "head"),
        P("seq", "head"),
        P("seq", "head"),
        P("seq", "head"),
        P("seq", None, "head"),
        P("seq", None, "head"),
    )
    return jax.shard_map(
        per_device,
        mesh=mesh,
        in_specs=placed,
        out_specs=(P(None, "seq", "head"), P(None, "seq", "head")),
        check_vma=False,
    )
```

profile of v0, /device:TPU:2, one launch (start us, length us, event | category | flops | bytes accessed | tf_op | source)
XLA Modules:
  0.0 919.2 jit_solution(8133665721481068145)
XLA Ops:
  13.3 80.1 %all-gather.10.cloned.1.call-done = bf16[5120,384]{1,0:T(8,128)(2,1)} async-done(((bf16[160,384]{1,0:T(8,128)(2,1)}), bf16[5120,384]{1,0:T(8,128)(2,1)}) %all-gather.10.cloned.1.call-update) | async-done | bytes 3932176 | tf_op jit(solution)/shard_map/all_gather | solution.py:57
  93.4 6.3 copy.77
  99.7 74.6 %all-gather.6.cloned.1.call-done = bf16[5120,384]{1,0:T(8,128)(2,1)} async-done(((bf16[160,384]{1,0:T(8,128)(2,1)}), bf16[5120,384]{1,0:T(8,128)(2,1)}) %all-gather.6.cloned.1.call-update) | async-done | bytes 3932176 | tf_op jit(solution)/shard_map/all_gather | solution.py:56
  174.3 6.3 copy.75
  180.6 3.5 fusion.59
  193.9 61.3 %all-gather.12.cloned.1.call-done = bf16[5120,384]{1,0:T(8,128)(2,1)} async-done(((bf16[160,384]{1,0:T(8,128)(2,1)}), bf16[5120,384]{1,0:T(8,128)(2,1)}) %all-gather.12.cloned.1.call-update) | async-done | bytes 3932176 | tf_op jit(solution)/shard_map/all_gather | solution.py:58
  255.2 6.3 copy.79
  262.2 4.0 convolution_convert_fusion
  266.2 69.3 %all-gather.8.cloned.1.call-done = bf16[2,8,256,3,128]{4,2,3,1,0:T(8,128)(2,1)} async-done(((bf16[2,8,8,3,128]{4,2,3,1,0:T(8,128)(2,1)}), bf16[2,8,256,3,128]{4,2,3,1,0:T(8,128)(2,1)}) %all-gather.8.cloned.1.call-update) | async-done | bytes 3145744 | tf_op jit(solution)/shard_map/all_gather | solution.py:73
  335.5 82.3 %while.16 = (s32[]{:T(128)}, f32[2,8,256,3]{2,1,3,0:T(8,128)}, f32[2,8,256,3]{2,1,3,0:T(8,128)}, f32[2,8,256,3,128]{4,2,3,1,0:T(8,128)}, s32[16]{0:T(128)S(1)}, ...) while((s32[]{:T(128)}, f32[2,8,256,3]{2,1,3,0:T(8,128)}, ...), condition=%wide.region_9.10_spmd.clone.clone, body=%wide.region_3.9_spmd.clone.clone.sunk | while | flops 1071998720 | bytes 124305208 | solution.py:144
  337.0 2.7 gather_fusion
  339.8 3.0 bitcast_reduce_fusion.2
  346.8 8.2 bitcast_multiply_fusion.4
  362.2 11.2 %fusion.103 = f32[1,8,256,3,128]{4,1,3,2,0:T(8,128)S(1)} fusion(f32[8,3,128,256]{2,0,1,3:T(8,128)} %copy.126, f32[16,256,3,128]{3,1,2,0:T(8,128)} %bitcast_multiply_fusion.4, f32[8,256,3]{0,2,1:T(4,128)} %copy.127, f32[8,256,3]{0,2,1:T(4,128)} %copy.128, s32[16]{0:T(128)S(1)} %get-tuple-element.340), kind=kOutput, calls=%fused_computation.19.clone.1 | convolution fusion | flops 153354496 | bytes 12632128 | tf_op jit(solution)/shard_map/while/body/eval_jaxpr/pr,pqhd->rqhd/dot_general | solution.py:116
  380.9 3.0 bitcast_reduce_fusion.2
  387.9 8.2 bitcast_multiply_fusion.4
  403.4 11.2 %fusion.103 = f32[1,8,256,3,128]{4,1,3,2,0:T(8,128)S(1)} fusion(f32[8,3,128,256]{2,0,1,3:T(8,128)} %copy.126, f32[16,256,3,128]{3,1,2,0:T(8,128)} %bitcast_multiply_fusion.4, f32[8,256,3]{0,2,1:T(4,128)} %copy.127, f32[8,256,3]{0,2,1:T(4,128)} %copy.128, s32[16]{0:T(128)S(1)} %get-tuple-element.340), kind=kOutput, calls=%fused_computation.19.clone.1 | convolution fusion | flops 153354496 | bytes 12632128 | tf_op jit(solution)/shard_map/while/body/eval_jaxpr/pr,pqhd->rqhd/dot_general | solution.py:116
  417.8 137.8 %pmax.7 = f32[2,8,256,3]{2,1,3,0:T(8,128)S(1)} all-reduce(f32[2,8,256,3]{2,1,3,0:T(8,128)} %get-tuple-element.72), channel_id=1, replica_groups=mesh['seq'=32,'head'=8] {'seq'}, use_global_device_ids=true, to_apply=%region_10.11 | all-reduce | flops 12288 | bytes 98304 | tf_op jit(solution)/shard_map/pmax | solution.py:145
  556.5 7.3 broadcast_multiply_fusion
  565.7 140.1 %all-reduce = f32[2,8,256,3]{2,1,3,0:T(8,128)S(1)} all-reduce(f32[2,8,256,3]{2,1,3,0:T(8,128)S(1)} %get-tuple-element.201), channel_id=3, replica_groups=mesh['seq'=32,'head'=8] {'seq'}, use_global_device_ids=true, to_apply=%region_12.13.clone | all-reduce | flops 12288 | bytes 98304
  706.0 82.0 %reduce-scatter.4.cloned.1.call-done = f32[2,8,8,3,128]{4,2,3,1,0:T(8,128)} async-done(((f32[2,8,256,3,128]{4,2,3,1,0:T(8,128)}), f32[2,8,8,3,128]{4,2,3,1,0:T(8,128)}) %reduce-scatter.4.cloned.1.call-update) | async-done | bytes 196624 | tf_op jit(solution)/shard_map/reduce_scatter | solution.py:148
  789.1 80.8 %all-gather.14.cloned.1.call-done = bf16[5120,384]{1,0:T(8,128)(2,1)} async-done(((bf16[160,384]{1,0:T(8,128)(2,1)}), bf16[5120,384]{1,0:T(8,128)(2,1)}) %all-gather.14.cloned.1.call-update) | async-done | bytes 3932176 | tf_op jit(solution)/shard_map/all_gather | solution.py:59
  869.8 5.0 fusion.66
  874.8 35.8 %reduce-scatter.6.cloned.1.call-done = f32[128,640]{1,0:T(8,128)} async-done(((f32[128,5120]{1,0:T(8,128)}), f32[128,640]{1,0:T(8,128)}) %reduce-scatter.6.cloned.1.call-update) | async-done | bytes 327696 | tf_op jit(solution)/shard_map/reduce_scatter | solution.py:157
  (136 shorter events, 55.7 us)
Async XLA Ops:
  7.2 5.8 copy-start.13
  7.2 86.2 %all-gather.10.cloned.1.call-start = ((), (), s32[]{:S(2)}) async-start(), calls=%async_computation.4 | async-start | bytes 4055040 | tf_op jit(solution)/shard_map/all_gather | solution.py:57
  7.9 166.4 %all-gather.6.cloned.1.call-start = ((), (), s32[]{:S(2)}) async-start(), calls=%async_computation.2 | async-start | bytes 4055040 | tf_op jit(solution)/shard_map/all_gather | solution.py:56
  8.7 246.5 %all-gather.12.cloned.1.call-start = ((), (), s32[]{:S(2)}) async-start(), calls=%async_computation.5 | async-start | bytes 4055040 | tf_op jit(solution)/shard_map/all_gather | solution.py:58
  9.4 326.1 %all-gather.8.cloned.1.call-start = ((), (), s32[]{:S(2)}) async-start(), calls=%async_computation.3 | async-start | bytes 3244032 | tf_op jit(solution)/shard_map/all_gather | solution.py:73
  174.3 6.3 copy-start.3
  174.3 6.3 copy-start.12
  180.6 3.5 copy-start.2
  186.4 601.6 %reduce-scatter.4.cloned.1.call-start = ((), (), s32[]{:S(2)}) async-start(), calls=%async_computation.6 | async-start | bytes 6488064 | tf_op jit(solution)/shard_map/reduce_scatter | solution.py:148
  190.0 3.6 copy-start.11
  337.0 2.8 copy-start.4
  342.8 2.6 copy-start
  346.8 8.2 copy-start.1
  346.8 8.2 copy-start.6
  373.4 2.3 copy-start.9
  373.4 2.5 copy-start.7
  378.2 2.8 copy-start.4
  383.9 2.6 copy-start
  387.9 8.3 copy-start.1
  387.9 8.3 copy-start.6
  414.6 2.4 copy-start.9
  414.6 2.6 copy-start.7
  563.9 306.0 %all-gather.14.cloned.1.call-start = ((), (), s32[]{:S(2)}) async-start(), calls=%async_computation.7 | async-start | bytes 4055040 | tf_op jit(solution)/shard_map/all_gather | solution.py:59
  564.4 346.2 %reduce-scatter.6.cloned.1.call-start = ((), (), s32[]{:S(2)}) async-start(), calls=%async_computation.8 | async-start | bytes 2949120 | tf_op jit(solution)/shard_map/reduce_scatter | solution.py:157
  (7 other events, 6.0 us)
Sparse Core Ops, SparseCore 0:
  10.6 82.7 all-gather.9
  96.0 78.2 all-gather.5
  176.9 78.2 all-gather.11
  257.5 77.9 all-gather.7
  564.0 223.9 reduce-scatter.3
  790.8 79.0 all-gather.13
  874.9 35.6 reduce-scatter.5
where the time goes:
time: 920 us; the launch traced here: 919 us
  waiting for transfers between devices  487 us (53%)
  blocking collectives  278 us (30%)
  matrix products  64.6 us (7%)
  local copies, waits for them, and re-layouts  53.1 us (6%)
  other arithmetic  21.4 us (2%)
  between operations  14.9 us (2%)
    unnamed x1, blocking collectives  140 us
    pmax x1, blocking collectives, per_device(): overall = lax.pmax(row_peak, 'seq')  138 us
    reduce_scatter x1, waiting for transfers between devices, per_device(): lax.psum_scatter(row_out * rescale[..., None], 'seq', scatter_dimension=2...  82 us
    all_gather x1, waiting for transfers between devices, per_device(): lax.all_gather(w_out, 'seq', axis=0, tiled=True)  80.8 us
    all_gather x1, waiting for transfers between devices, per_device(): lax.all_gather(w_key, 'seq', axis=0, tiled=True)  80.1 us
    all_gather x1, waiting for transfers between devices, per_device(): lax.all_gather(w_query, 'seq', axis=0, tiled=True)  74.6 us
    all_gather x1, waiting for transfers between devices, per_device(): every_query = lax.all_gather(new_queries, 'seq', axis=2, tiled=True)  69.3 us
    all_gather x1, waiting for transfers between devices, per_device(): lax.all_gather(w_value, 'seq', axis=0, tiled=True)  61.3 us
  transfers between devices with their start and end apart: 7, of which 7 were waited for; matrix products, arithmetic and copies ran while one was open for 5% of the time, Pallas kernels for 0%

commit v1 on v0

--- a/solution.py
+++ b/solution.py
@@ -70,7 +70,8 @@
     new_queries = rotate(query_rows.reshape(shaped), positions).astype(jnp.bfloat16)
     new_keys = rotate(key_rows.reshape(shaped), positions).astype(jnp.bfloat16)
     new_values = value_rows.reshape(shaped).astype(jnp.bfloat16)
-    every_query = lax.all_gather(new_queries, "seq", axis=2, tiled=True)
+    sent = jnp.stack([new_queries] * lax.axis_size("seq"))
+    every_query = jnp.concatenate(lax.all_to_all(sent, "seq", 0, 0), axis=2)
     pages_here = key_cache.shape[0]
     page_ids = seq_place * pages_here + jnp.arange(pages_here, dtype=jnp.int32)
     table_slots = jnp.arange(page_table.shape[0], dtype=jnp.int32)

time: 920 us -> 886 us (0.963)
  waiting for transfers between devices: 487 us -> 437 us
    all_gather x1 -> x0, waiting for transfers between devices: 69.3 us -> none  [per_device(): every_query = lax.all_gather(new_queries, 'seq', axis=2, tiled=True)]
    all_gather x1, waiting for transfers between devices: 61.3 us -> 79.8 us  [per_device(): lax.all_gather(w_value, 'seq', axis=0, tiled=True)]
  transfers between devices with their start and end apart: 7 -> 7, of which waited for: 7 -> 6; matrix products, arithmetic and copies ran while one was open for 5% -> 5% of each run, Pallas kernels for 0% -> 0%
where the time goes in v1:
time: 886 us; the launch traced here: 885 us
  waiting for transfers between devices  437 us (49%)
  blocking collectives  277 us (31%)
  matrix products  65 us (7%)
  local copies, waits for them, and re-layouts  61.4 us (7%)
  other arithmetic  21 us (2%)
  between operations  14.9 us (2%)
    unnamed x1, blocking collectives  140 us
    pmax x1, blocking collectives, per_device(): overall = lax.pmax(row_peak, 'seq')  137 us
    reduce_scatter x1, waiting for transfers between devices, per_device(): lax.psum_scatter(row_out * rescale[..., None], 'seq', scatter_dimension=2...  83.6 us
    all_gather x1, waiting for transfers between devices, per_device(): lax.all_gather(w_out, 'seq', axis=0, tiled=True)  80.7 us
    all_gather x1, waiting for transfers between devices, per_device(): lax.all_gather(w_key, 'seq', axis=0, tiled=True)  79.9 us
    all_gather x1, waiting for transfers between devices, per_device(): lax.all_gather(w_value, 'seq', axis=0, tiled=True)  79.8 us
    all_gather x1, waiting for transfers between devices, per_device(): lax.all_gather(w_query, 'seq', axis=0, tiled=True)  74.6 us
    reduce_scatter x1, waiting for transfers between devices, per_device(): lax.psum_scatter(partial_value, 'head', scatter_dimension=1, tiled=True)  35.9 us
  transfers between devices with their start and end apart: 7, of which 6 were waited for; matrix products, arithmetic and copies ran while one was open for 5% of the time, Pallas kernels for 0%

profile of v1, /device:TPU:2, one launch (start us, length us, event | category | flops | bytes accessed | tf_op | source)
XLA Modules:
  0.0 884.6 jit_solution(8730756467640048298)
XLA Ops:
  13.5 79.9 %all-gather.7.cloned.1.call-done = bf16[5120,384]{1,0:T(8,128)(2,1)} async-done(((bf16[160,384]{1,0:T(8,128)(2,1)}), bf16[5120,384]{1,0:T(8,128)(2,1)}) %all-gather.7.cloned.1.call-update) | async-done | bytes 3932176 | tf_op jit(solution)/shard_map/all_gather | solution.py:57
  93.4 6.3 copy.100
  99.7 74.6 %all-gather.5.cloned.1.call-done = bf16[5120,384]{1,0:T(8,128)(2,1)} async-done(((bf16[160,384]{1,0:T(8,128)(2,1)}), bf16[5120,384]{1,0:T(8,128)(2,1)}) %all-gather.5.cloned.1.call-update) | async-done | bytes 3932176 | tf_op jit(solution)/shard_map/all_gather | solution.py:56
  174.3 6.3 copy.97
  180.6 3.5 fusion.59
  188.1 7.3 all-to-all-start
  206.2 79.8 %all-gather.9.cloned.1.call-done = bf16[5120,384]{1,0:T(8,128)(2,1)} async-done(((bf16[160,384]{1,0:T(8,128)(2,1)}), bf16[5120,384]{1,0:T(8,128)(2,1)}) %all-gather.9.cloned.1.call-update) | async-done | bytes 3932176 | tf_op jit(solution)/shard_map/all_gather | solution.py:58
  286.0 6.3 copy.102
  293.0 4.4 convolution_convert_fusion
  300.0 82.3 %while.16 = (s32[]{:T(128)}, f32[2,8,256,3]{2,1,3,0:T(8,128)}, f32[2,8,256,3]{2,1,3,0:T(8,128)}, f32[2,8,256,3,128]{4,2,3,1,0:T(8,128)}, s32[16]{0:T(128)S(1)}, ...) while((s32[]{:T(128)}, f32[2,8,256,3]{2,1,3,0:T(8,128)}, ...), condition=%wide.region_9.10_spmd.clone.clone, body=%wide.region_3.9_spmd.clone.clone.sunk | while | flops 1071998720 | bytes 124305208 | solution.py:145
  304.3 3.0 bitcast_reduce_fusion.2
  311.3 8.2 bitcast_multiply_fusion.4
  326.8 11.2 %fusion.103 = f32[1,8,256,3,128]{4,1,3,2,0:T(8,128)S(1)} fusion(f32[8,3,128,256]{2,0,1,3:T(8,128)} %copy.151, f32[16,256,3,128]{3,1,2,0:T(8,128)} %bitcast_multiply_fusion.4, f32[8,256,3]{0,2,1:T(4,128)} %copy.152, f32[8,256,3]{0,2,1:T(4,128)} %copy.153, s32[16]{0:T(128)S(1)} %get-tuple-element.352), kind=kOutput, calls=%fused_computation.19.clone.1 | convolution fusion | flops 153354496 | bytes 12632128 | tf_op jit(solution)/shard_map/while/body/eval_jaxpr/pr,pqhd->rqhd/dot_general | solution.py:117
  342.7 2.7 gather_fusion
  345.4 3.0 bitcast_reduce_fusion.2
  352.4 8.2 bitcast_multiply_fusion.4
  367.9 11.2 %fusion.103 = f32[1,8,256,3,128]{4,1,3,2,0:T(8,128)S(1)} fusion(f32[8,3,128,256]{2,0,1,3:T(8,128)} %copy.151, f32[16,256,3,128]{3,1,2,0:T(8,128)} %bitcast_multiply_fusion.4, f32[8,256,3]{0,2,1:T(4,128)} %copy.152, f32[8,256,3]{0,2,1:T(4,128)} %copy.153, s32[16]{0:T(128)S(1)} %get-tuple-element.352), kind=kOutput, calls=%fused_computation.19.clone.1 | convolution fusion | flops 153354496 | bytes 12632128 | tf_op jit(solution)/shard_map/while/body/eval_jaxpr/pr,pqhd->rqhd/dot_general | solution.py:117
  382.3 136.9 %pmax.7 = f32[2,8,256,3]{2,1,3,0:T(8,128)S(1)} all-reduce(f32[2,8,256,3]{2,1,3,0:T(8,128)} %get-tuple-element.72), channel_id=1, replica_groups=mesh['seq'=32,'head'=8] {'seq'}, use_global_device_ids=true, to_apply=%region_10.11 | all-reduce | flops 12288 | bytes 98304 | tf_op jit(solution)/shard_map/pmax | solution.py:146
  520.1 7.3 broadcast_multiply_fusion
  529.3 140.4 %all-reduce = f32[2,8,256,3]{2,1,3,0:T(8,128)S(1)} all-reduce(f32[2,8,256,3]{2,1,3,0:T(8,128)S(1)} %get-tuple-element.213), channel_id=3, replica_groups=mesh['seq'=32,'head'=8] {'seq'}, use_global_device_ids=true, to_apply=%region_12.13.clone | all-reduce | flops 12288 | bytes 98304
  669.8 83.6 %reduce-scatter.4.cloned.1.call-done = f32[2,8,8,3,128]{4,2,3,1,0:T(8,128)} async-done(((f32[2,8,256,3,128]{4,2,3,1,0:T(8,128)}), f32[2,8,8,3,128]{4,2,3,1,0:T(8,128)}) %reduce-scatter.4.cloned.1.call-update) | async-done | bytes 196624 | tf_op jit(solution)/shard_map/reduce_scatter | solution.py:149
  754.5 80.7 %all-gather.11.cloned.1.call-done = bf16[5120,384]{1,0:T(8,128)(2,1)} async-done(((bf16[160,384]{1,0:T(8,128)(2,1)}), bf16[5120,384]{1,0:T(8,128)(2,1)}) %all-gather.11.cloned.1.call-update) | async-done | bytes 3932176 | tf_op jit(solution)/shard_map/all_gather | solution.py:59
  835.2 5.0 fusion.66
  840.2 35.9 %reduce-scatter.6.cloned.1.call-done = f32[128,640]{1,0:T(8,128)} async-done(((f32[128,5120]{1,0:T(8,128)}), f32[128,640]{1,0:T(8,128)}) %reduce-scatter.6.cloned.1.call-update) | async-done | bytes 327696 | tf_op jit(solution)/shard_map/reduce_scatter | solution.py:158
  (139 shorter events, 63.6 us)
Async XLA Ops:
  7.2 6.0 copy-start.14
  7.2 86.2 %all-gather.7.cloned.1.call-start = ((), (), s32[]{:S(2)}) async-start(), calls=%async_computation.4 | async-start | bytes 4055040 | tf_op jit(solution)/shard_map/all_gather | solution.py:57
  7.9 166.4 %all-gather.5.cloned.1.call-start = ((), (), s32[]{:S(2)}) async-start(), calls=%async_computation.3 | async-start | bytes 4055040 | tf_op jit(solution)/shard_map/all_gather | solution.py:56
  8.7 277.4 %all-gather.9.cloned.1.call-start = ((), (), s32[]{:S(2)}) async-start(), calls=%async_computation.5 | async-start | bytes 4055040 | tf_op jit(solution)/shard_map/all_gather | solution.py:58
  11.5 172.6 %copy-start.4 = (bf16[1,8,8,5120]{3,2,1,0:T(8,128)(2,1)}, bf16[1,8,8,5120]{3,2,1,0:T(8,128)(2,1)S(1)}, u32[]{:S(2)}) copy-start(bf16[1,8,8,5120]{3,2,1,0:T(8,128)(2,1)S(1)} %select_bitcast_fusion) | copy-start | bytes 1966084
  174.3 6.3 copy-start.3
  174.3 6.3 copy-start.13
  180.6 3.6 copy-start.2
  188.1 109.3 %all-to-all-start = ((bf16[32,2,8,8,3,128]{5,3,4,2,1,0:T(8,128)(2,1)}), bf16[32,2,8,8,3,128]{5,3,4,2,1,0:T(8,128)(2,1)S(1)}, u32[]{:S(2)}, u32[]{:S(2)}) async-start(bf16[32,2,8,8,3,128]{5,3,4,2,1,0:T(8,128)(2,1)} %stack.11), calls=%async_computation | async-start | bytes 6291456 | tf_op jit(solution)/shard_map/all_to_all | solution.py:74
  195.4 558.0 %reduce-scatter.4.cloned.1.call-start = ((), (), s32[]{:S(2)}) async-start(), calls=%async_computation.6 | async-start | bytes 6488064 | tf_op jit(solution)/shard_map/reduce_scatter | solution.py:149
  200.7 5.2 copy-start.12
  301.6 2.8 copy-start.5
  307.3 2.6 copy-start
  311.3 8.3 copy-start.1
  311.3 8.3 copy-start.7
  338.0 2.5 copy-start.8
  342.7 2.8 copy-start.5
  348.4 2.6 copy-start
  352.4 8.2 copy-start.1
  352.4 8.2 copy-start.7
  379.1 2.4 copy-start.10
  379.1 2.6 copy-start.8
  527.4 307.8 %all-gather.11.cloned.1.call-start = ((), (), s32[]{:S(2)}) async-start(), calls=%async_computation.7 | async-start | bytes 4055040 | tf_op jit(solution)/shard_map/all_gather | solution.py:59
  528.0 348.1 %reduce-scatter.6.cloned.1.call-start = ((), (), s32[]{:S(2)}) async-start(), calls=%async_computation.8 | async-start | bytes 2949120 | tf_op jit(solution)/shard_map/reduce_scatter | solution.py:158
  (8 other events, 8.3 us)
Sparse Core Ops, SparseCore 0:
  10.6 82.7 all-gather.6
  96.0 78.2 all-gather.4
  176.9 109.1 all-gather.8
  527.5 225.8 reduce-scatter.3
  756.2 78.9 all-gather.10
  840.3 35.7 reduce-scatter.5
